TPU v7x, 32 devices: a whole 2x2x4 slice. The times are simulated.
32 devices in a mesh: grp: 4 (over y, x), freq: 8 (over z, core).
Axes of the slice: x: 2, y: 2, z: 4, core: 2. Of those that a mesh axis runs over, the one named last changes fastest.
Arguments:
- transfer: bfloat16 [512, 2, 128, 512], P('freq', None, 'grp'), may hold values from -0.1875 to 0.1875
- adjoint: bfloat16 [512, 2, 512, 128], P('freq'), may hold values from -6 to 6
- lower_rows: bfloat16 [131072, 384], P(('grp', 'freq')), may hold values from -6 to 6
- pivot_store: bfloat16 [512, 384], P('grp'), may hold values from -0.3125 to 0.3125
- owners: int32 [3], replicated, may hold values from 0 to 3
- inverse_factor: bfloat16 [128, 128], replicated, as said below
Outputs:
- panel: bfloat16 [131072, 128], P(('grp', 'freq'))
Inputs may be any that keep to these rules, and one draw needn't show every extreme that they name: `inverse_factor`: upper triangular, with diagonal entries from 0.5 to 2.
All inputs are finite; a program needn't handle non-finite values.
Results may differ from a plain program's by a relative error of at most 0.0059.
Values may be sent and summed in bfloat16 or wider, within the bound.
A program may use at most 64 MiB of HBM per device.

v0:
```python
import math
import jax
import jax.numpy as jnp
from jax import lax
from jax.sharding import PartitionSpec as P

C = 128
NF = 512
PANELS = 3
NT = 1024


def make_table(samples, frequencies):
    time_steps = jnp.arange(samples, dtype=jnp.int32)[:, None]
    wave_numbers = jnp.arange(frequencies, dtype=jnp.int32)[None, :]
    phases = (time_steps * wave_numbers % samples).astype(jnp.float32) * (2.0 * math.pi / samples)
    factor = 1.0 / math.sqrt(frequencies)
    return jnp.stack([jnp.cos(phases) * factor, -jnp.sin(phases) * factor]).astype(jnp.bfloat16)


def product(left, right):
    return jnp.einsum("ksm,kmc->ksc", left, right, preferred_element_type=jnp.float32)


def per_device(transfer, adjoint, lower_rows, pivot_store, owners, inverse_factor):
    trans_real = transfer[:, 0]
    trans_imag = transfer[:, 1]
    adjoint_real = adjoint[:, 0]
    adjoint_imag = adjoint[:, 1]
    real_part = product(trans_real, adjoint_real) - product(trans_imag, adjoint_imag)
    imag_part = product(trans_real, adjoint_imag) + product(trans_imag, adjoint_real)
    spectra = jnp.stack([real_part, imag_part], axis=2).astype(jnp.bfloat16)
    table = make_table(NT, NF)
    hessian = jnp.einsum(
        "qtk,ksqc->stc",
        table,
        lax.all_to_all(spectra, "freq", split_axis=1, concat_axis=0, tiled=True),
        preferred_element_type=jnp.float32,
    )
    hessian = hessian.reshape(-1, hessian.shape[-1])
    owned_mask = (owners == lax.axis_index("grp")).astype(jnp.float32)
    local_blocks = pivot_store.reshape(C, PANELS, C).astype(jnp.float32) * owned_mask[None, :, None]
    combined = lax.psum(local_blocks.astype(jnp.bfloat16), "grp")
    pivots = combined.reshape(C, PANELS * C)
    update = lax.dot_general(
        lower_rows, pivots, (((1,), (1,)), ((), ())), preferred_element_type=jnp.float32
    )
    reduced = (hessian - update).astype(jnp.bfloat16)
    return jnp.dot(reduced, inverse_factor, preferred_element_type=jnp.float32).astype(jnp.bfloat16)


def solution(mesh):
    in_specs = (
        P("freq", None, "grp", None),
        P("freq", None, None, None),
        P(("grp", "freq"), None),
        P("grp", None),
        P(),
        P(),
    )
    out_specs = P(("grp", "freq"), None)
    return jax.shard_map(
        per_device, mesh=mesh, in_specs=in_specs, out_specs=out_specs, check_vma=False
    )
```

profile of v0, /device:TPU:0, one launch (start us, length us, event | category | flops | bytes accessed | tf_op | source)
XLA Modules:
  0.0 87.9 jit_solution(477097812663604727)
XLA Ops:
  6.5 5.5 %fusion.2 = f32[64,32,128]{2,1,0:T(8,128)S(1)} fusion(bf16[64,2,512,128]{3,2,1,0:T(8,128)(2,1)} %param.7, bf16[64,2,32,512]{3,2,1,0:T(8,128)(2,1)} %param.6), kind=kOutput, calls=%fused_computation.2 | convolution fusion | flops 268435456 | bytes 11534336 | tf_op jit(solution)/shard_map/ksm,kmc->ksc/dot_general | solution.py:22
  12.0 5.5 %fusion = f32[64,32,128]{2,1,0:T(8,128)S(1)} fusion(bf16[64,2,512,128]{3,2,1,0:T(8,128)(2,1)} %param.7, bf16[64,2,32,512]{3,2,1,0:T(8,128)(2,1)S(1)} %copy-done.6), kind=kOutput, calls=%fused_computation | convolution fusion | flops 268435456 | bytes 11534336 | tf_op jit(solution)/shard_map/ksm,kmc->ksc/dot_general | solution.py:22
  17.6 1.5 %copy-done.5 = bf16[64,2,512,128]{3,2,1,0:T(8,128)(2,1)S(1)} copy-done((bf16[64,2,512,128]{3,2,1,0:T(8,128)(2,1)S(1)}, bf16[64,2,512,128]{3,2,1,0:T(8,128)(2,1)}, u32[]{:S(2)}) %copy-start.5) | copy-done | bytes 16777240
  19.1 1.4 %fusion.52 = bf16[64,32,1,128]{3,1,0,2:T(8,128)(2,1)S(1)} fusion(f32[64,32,128]{2,1,0:T(8,128)S(1)} %fusion.2, bf16[64,2,512,128]{3,2,1,0:T(8,128)(2,1)S(1)} %copy-done.5, bf16[64,2,32,512]{3,2,1,0:T(8,128)(2,1)S(1)} %copy-done.6), kind=kOutput, calls=%fused_computation.44 | convolution fusion | flops 268959744 | bytes 12058624 | tf_op jit(solution)/shard_map/ksm,kmc->ksc/dot_general | solution.py:22
  20.5 1.4 %fusion.57 = bf16[64,32,1,128]{3,1,0,2:T(8,128)(2,1)S(1)} fusion(f32[64,32,128]{2,1,0:T(8,128)S(1)} %fusion, bf16[64,2,512,128]{3,2,1,0:T(8,128)(2,1)S(1)} %copy-done.5, bf16[64,2,32,512]{3,2,1,0:T(8,128)(2,1)S(1)} %copy-done.6), kind=kOutput, calls=%fused_computation.45 | convolution fusion | flops 268959744 | bytes 12058624 | tf_op jit(solution)/shard_map/ksm,kmc->ksc/dot_general | solution.py:22
  21.9 0.1 pad_maximum_fusion
  22.0 0.0 copy-start.3
  22.0 0.0 copy-start.7
  22.0 1.4 %copy.33 = bf16[64,32,2,128]{3,0,2,1:T(8,128)(2,1)} copy(bf16[64,32,2,128]{3,1,0,2:T(8,128)(2,1)S(1)} %pad_maximum_fusion) | data formatting | bytes 2097152 | tf_op jit(solution)/shard_map/stack | solution.py:32
  23.4 6.4 %all-to-all-start = ((bf16[64,32,2,128]{3,0,2,1:T(8,128)(2,1)}), bf16[64,32,2,128]{3,0,2,1:T(8,128)(2,1)}, u32[]{:S(2)}, u32[]{:S(2)}) async-start(bf16[64,32,2,128]{3,0,2,1:T(8,128)(2,1)} %copy.33), calls=%async_computation | async-start | bytes 2097152 | tf_op jit(solution)/shard_map/all_to_all | solution.py:37
  29.7 0.0 all-reduce.2.cloned.1.call-start
  29.8 0.1 copy.37
  29.9 0.7 fusion.62
  30.7 0.0 all-reduce.2.cloned.1.call-update
  30.7 9.3 %multiply_convert_fusion = (bf16[1,1024,512]{2,1,0:T(8,128)(2,1)}, bf16[1,1024,512]{2,1,0:T(8,128)(2,1)}) fusion(), kind=kLoop, calls=%fused_computation.30 | loop fusion | flops 9961472 | bytes 2097152 | tf_op jit(solution)/shard_map/convert.2
  40.0 16.4 %all-to-all-done = bf16[64,32,2,128]{3,0,2,1:T(8,128)(2,1)} async-done(((bf16[64,32,2,128]{3,0,2,1:T(8,128)(2,1)}), bf16[64,32,2,128]{3,0,2,1:T(8,128)(2,1)}, u32[]{:S(2)}, u32[]{:S(2)}) %all-to-all-start) | async-done | bytes 1048608 | tf_op jit(solution)/shard_map/all_to_all | solution.py:37
  56.4 1.4 %copy.34 = bf16[8,64,4,2,128]{4,1,0,3,2:T(8,128)(2,1)S(1)} copy(bf16[8,64,4,2,128]{4,1,3,2,0:T(8,128)(2,1)} %bitcast.7) | data formatting | bytes 2097152 | tf_op jit(solution)/shard_map/all_to_all | solution.py:37
  57.9 0.1 copy-done.1
  57.9 0.3 copy-done.2
  58.3 2.6 %fusion.31 = f32[4,1024,128]{1,2,0:T(8,128)} fusion(bf16[512,4,2,128]{3,0,2,1:T(8,128)(2,1)S(1)} %bitcast.87, bf16[1,1024,512]{2,1,0:T(8,128)(2,1)S(1)} %copy-done.1, bf16[1,1024,512]{2,1,0:T(8,128)(2,1)S(1)} %copy-done.2), kind=kOutput, calls=%fused_computation.39 | convolution fusion | flops 1074790400 | bytes 5242880 | tf_op jit(solution)/shard_map/qtk,ksqc->stc/dot_general | solution.py:34
  60.9 2.9 %copy.36 = f32[4,1024,128]{2,1,0:T(8,128)} copy(f32[4,1024,128]{1,2,0:T(8,128)} %fusion.31) | data formatting | bytes 4194304 | tf_op jit(solution)/shard_map/qtk,ksqc->stc/transpose | solution.py:34
  63.8 2.9 %copy.38 = f32[4096,128]{0,1:T(8,128)} copy(f32[4096,128]{1,0:T(8,128)} %bitcast.86) | data formatting | bytes 4194304 | tf_op jit(solution)/shard_map/reshape | solution.py:40
  66.7 10.3 %all-reduce.2.cloned.1.call-done = bf16[128,384]{0,1:T(8,128)(2,1)} async-done(((bf16[128,384]{0,1:T(8,128)(2,1)}), bf16[128,384]{0,1:T(8,128)(2,1)}) %all-reduce.2.cloned.1.call-update) | async-done | bytes 98320 | tf_op jit(solution)/shard_map/psum | solution.py:43
  77.0 4.1 %convolution_convert_fusion = bf16[4096,128]{1,0:T(8,128)(2,1)} fusion(bf16[128,128]{1,0:T(8,128)(2,1)S(1)} %copy-done.4, f32[4096,128]{0,1:T(8,128)} %copy.38, bf16[128,384]{0,1:T(8,128)(2,1)} %all-reduce.2.cloned.1.call-done, bf16[4096,384]{1,0:T(8,128)(2,1)S(1)} %copy-done), kind=kOutput, calls=%fused_computation.15 | convolution fusion | flops 538443776 | bytes 6422528 | tf_op jit(solution)/shard_map/dot_general | solution.py:49
  (12 shorter events, 0.0 us)
Async XLA Ops:
  6.5 70.5 %copy-start = (bf16[4096,384]{1,0:T(8,128)(2,1)S(1)}, bf16[4096,384]{1,0:T(8,128)(2,1)}, u32[]{:S(2)}) copy-start(bf16[4096,384]{1,0:T(8,128)(2,1)} %param.8) | copy-start | bytes 9437188
  6.5 5.5 %copy-start.6 = (bf16[64,2,32,512]{3,2,1,0:T(8,128)(2,1)S(1)}, bf16[64,2,32,512]{3,2,1,0:T(8,128)(2,1)}, u32[]{:S(2)}) copy-start(bf16[64,2,32,512]{3,2,1,0:T(8,128)(2,1)} %param.6) | copy-start | bytes 12582916
  6.5 12.6 %copy-start.5 = (bf16[64,2,512,128]{3,2,1,0:T(8,128)(2,1)S(1)}, bf16[64,2,512,128]{3,2,1,0:T(8,128)(2,1)}, u32[]{:S(2)}) copy-start(bf16[64,2,512,128]{3,2,1,0:T(8,128)(2,1)} %param.7) | copy-start | bytes 50331652
  22.0 7.8 %copy-start.3 = (bf16[128,384]{1,0:T(8,128)(2,1)S(1)}, bf16[128,384]{1,0:T(8,128)(2,1)}, u32[]{:S(2)}) copy-start(bf16[128,384]{1,0:T(8,128)(2,1)} %param.9) | copy-start | bytes 294916
  22.0 7.9 %copy-start.7 = (s32[3]{0:T(128)S(1)}, s32[3]{0:T(128)}, u32[]{:S(2)}) copy-start(s32[3]{0:T(128)} %param.10) | copy-start | bytes 40
  23.4 33.0 %all-to-all-start = ((bf16[64,32,2,128]{3,0,2,1:T(8,128)(2,1)}), bf16[64,32,2,128]{3,0,2,1:T(8,128)(2,1)}, u32[]{:S(2)}, u32[]{:S(2)}) async-start(bf16[64,32,2,128]{3,0,2,1:T(8,128)(2,1)} %copy.33), calls=%async_computation | async-start | bytes 2097152 | tf_op jit(solution)/shard_map/all_to_all | solution.py:37
  29.7 47.3 %all-reduce.2.cloned.1.call-start = ((), (), s32[]{:S(2)}) async-start(), calls=%async_computation.1 | async-start | bytes 196608 | tf_op jit(solution)/shard_map/psum | solution.py:43
  56.4 1.5 %copy-start.1 = (bf16[1,1024,512]{2,1,0:T(8,128)(2,1)S(1)}, bf16[1,1024,512]{2,1,0:T(8,128)(2,1)}, u32[]{:S(2)}) copy-start(bf16[1,1024,512]{2,1,0:T(8,128)(2,1)} %get-tuple-element.5) | copy-start | bytes 3145732
  56.4 1.9 %copy-start.2 = (bf16[1,1024,512]{2,1,0:T(8,128)(2,1)S(1)}, bf16[1,1024,512]{2,1,0:T(8,128)(2,1)}, u32[]{:S(2)}) copy-start(bf16[1,1024,512]{2,1,0:T(8,128)(2,1)} %get-tuple-element.6) | copy-start | bytes 3145732
  63.8 13.2 %copy-start.4 = (bf16[128,128]{1,0:T(8,128)(2,1)S(1)}, bf16[128,128]{1,0:T(8,128)(2,1)}, u32[]{:S(2)}) copy-start(bf16[128,128]{1,0:T(8,128)(2,1)} %param.11) | copy-start | bytes 98308
Sparse Core Ops, SparseCore 0:
  33.4 43.5 all-reduce.1
where the time goes:
time: 88.2 us; the launch traced here: 87.9 us
  waiting for transfers between devices  26.7 us (30%)
  matrix products  20.4 us (23%)
  between operations  13.5 us (15%)
  local copies, waits for them, and re-layouts  10.7 us (12%)
  other arithmetic  10.2 us (12%)
  starting transfers between devices  6.39 us (7%)
    all_to_all x1, waiting for transfers between devices, per_device(): lax.all_to_all(spectra, 'freq', split_axis=1, concat_axis=0, tiled=True)  16.4 us
    dot_general x4, matrix products, product(): jnp.einsum('ksm,kmc->ksc', left, right, preferred_element_type=jnp.float32)  13.8 us
    psum x1, waiting for transfers between devices, per_device(): combined = lax.psum(local_blocks.astype(jnp.bfloat16), 'grp')  10.3 us
    another operation x1, other arithmetic  9.32 us
    all_to_all x1, starting transfers between devices, per_device(): lax.all_to_all(spectra, 'freq', split_axis=1, concat_axis=0, tiled=True)  6.35 us
    dot_general x1, matrix products, per_device(): jnp.dot(reduced, inverse_factor, preferred_element_type=jnp.float32)  4.05 us
    transpose x1, local copies, waits for them, and re-layouts, per_device(): jnp.einsum('qtk,ksqc->stc', table, lax.all_to_all(spectra, 'freq', split_...  2.91 us
    reshape x1, local copies, waits for them, and re-layouts, per_device(): hessian = hessian.reshape(-1, hessian.shape[-1])  2.91 us
  transfers between devices with their start and end apart: 2, of which 2 were waited for; matrix products, arithmetic and copies ran while one was open for 23% of the time, Pallas kernels for 0%

commit v1 on v0

--- a/solution.py
+++ b/solution.py
@@ -1,3 +1,4 @@
+import functools
 import math
 import jax
 import jax.numpy as jnp
@@ -8,6 +9,13 @@
 NF = 512
 PANELS = 3
 NT = 1024
+
+
+def view_knots(sheet, axis_id):
+    return lax.all_gather(sheet, axis_name=axis_id).sum(axis=0)
+
+
+map_windows_by_axis = functools.partial(view_knots, axis_id="grp")
 
 
 def make_table(samples, frequencies):
@@ -40,7 +48,7 @@
     hessian = hessian.reshape(-1, hessian.shape[-1])
     owned_mask = (owners == lax.axis_index("grp")).astype(jnp.float32)
     local_blocks = pivot_store.reshape(C, PANELS, C).astype(jnp.float32) * owned_mask[None, :, None]
-    combined = lax.psum(local_blocks.astype(jnp.bfloat16), "grp")
+    combined = map_windows_by_axis(local_blocks.astype(jnp.bfloat16))
     pivots = combined.reshape(C, PANELS * C)
     update = lax.dot_general(
         lower_rows, pivots, (((1,), (1,)), ((), ())), preferred_element_type=jnp.float32

time: 88.2 us -> 64.5 us (0.73)
  waiting for transfers between devices: 26.7 us -> 4.01 us
  between operations: 13.5 us -> 0.12 us
  blocking collectives: 0 us -> 10.6 us
  local copies, waits for them, and re-layouts: 10.7 us -> 12.5 us
    all_to_all x1, waiting for transfers between devices: 16.4 us -> 4.01 us  [per_device(): lax.all_to_all(spectra, 'freq', split_axis=1, concat_axis=0, tiled=True)]
    all_gather x0 -> x1, blocking collectives: none -> 10.6 us  [view_knots(): return lax.all_gather(sheet, axis_name=axis_id).sum(axis=0)]
    psum x1 -> x0, waiting for transfers between devices: 10.3 us -> none  [per_device(): combined = lax.psum(local_blocks.astype(jnp.bfloat16), 'grp')]
    reduce_sum x0 -> x1, local copies, waits for them, and re-layouts: none -> 1.01 us  [view_knots(): return lax.all_gather(sheet, axis_name=axis_id).sum(axis=0)]
  transfers between devices with their start and end apart: 2 -> 1, of which waited for: 2 -> 1; matrix products, arithmetic and copies ran while one was open for 23% -> 19% of each run, Pallas kernels for 0% -> 0%
where the time goes in v1:
time: 64.5 us; the launch traced here: 64.2 us
  matrix products  20.3 us (31%)
  local copies, waits for them, and re-layouts  12.5 us (19%)
  blocking collectives  10.6 us (16%)
  other arithmetic  10.3 us (16%)
  starting transfers between devices  6.35 us (10%)
  waiting for transfers between devices  4.01 us (6%)
    dot_general x4, matrix products, product(): jnp.einsum('ksm,kmc->ksc', left, right, preferred_element_type=jnp.float32)  13.8 us
    all_gather x1, blocking collectives, view_knots(): return lax.all_gather(sheet, axis_name=axis_id).sum(axis=0)  10.6 us
    another operation x1, other arithmetic  9.36 us
    all_to_all x1, starting transfers between devices, per_device(): lax.all_to_all(spectra, 'freq', split_axis=1, concat_axis=0, tiled=True)  6.35 us
    all_to_all x1, waiting for transfers between devices, per_device(): lax.all_to_all(spectra, 'freq', split_axis=1, concat_axis=0, tiled=True)  4.01 us
    dot_general x1, matrix products, per_device(): jnp.dot(reduced, inverse_factor, preferred_element_type=jnp.float32)  3.99 us
    transpose x1, local copies, waits for them, and re-layouts, per_device(): jnp.einsum('qtk,ksqc->stc', table, lax.all_to_all(spectra, 'freq', split_...  2.93 us
    reshape x1, local copies, waits for them, and re-layouts, per_device(): hessian = hessian.reshape(-1, hessian.shape[-1])  2.9 us
  transfers between devices with their start and end apart: 1, of which 1 were waited for; matrix products, arithmetic and copies ran while one was open for 19% of the time, Pallas kernels for 0%

profile of v1, /device:TPU:0, one launch (start us, length us, event | category | flops | bytes accessed | tf_op | source)
XLA Modules:
  0.0 64.2 jit_solution(8504760456058720791)
XLA Ops:
  0.0 5.5 %fusion.2 = f32[64,32,128]{2,1,0:T(8,128)S(1)} fusion(bf16[64,2,512,128]{3,2,1,0:T(8,128)(2,1)} %param.7, bf16[64,2,32,512]{3,2,1,0:T(8,128)(2,1)} %param.6), kind=kOutput, calls=%fused_computation.2 | convolution fusion | flops 268435456 | bytes 11534336 | tf_op jit(solution)/shard_map/ksm,kmc->ksc/dot_general | solution.py:30
  5.5 5.5 %fusion = f32[64,32,128]{2,1,0:T(8,128)S(1)} fusion(bf16[64,2,512,128]{3,2,1,0:T(8,128)(2,1)} %param.7, bf16[64,2,32,512]{3,2,1,0:T(8,128)(2,1)S(1)} %copy-done.6), kind=kOutput, calls=%fused_computation | convolution fusion | flops 268435456 | bytes 11534336 | tf_op jit(solution)/shard_map/ksm,kmc->ksc/dot_general | solution.py:30
  11.1 1.5 %copy-done.5 = bf16[64,2,512,128]{3,2,1,0:T(8,128)(2,1)S(1)} copy-done((bf16[64,2,512,128]{3,2,1,0:T(8,128)(2,1)S(1)}, bf16[64,2,512,128]{3,2,1,0:T(8,128)(2,1)}, u32[]{:S(2)}) %copy-start.5) | copy-done | bytes 16777240
  12.6 1.4 %fusion.52 = bf16[64,32,1,128]{3,1,0,2:T(8,128)(2,1)S(1)} fusion(f32[64,32,128]{2,1,0:T(8,128)S(1)} %fusion.2, bf16[64,2,512,128]{3,2,1,0:T(8,128)(2,1)S(1)} %copy-done.5, bf16[64,2,32,512]{3,2,1,0:T(8,128)(2,1)S(1)} %copy-done.6), kind=kOutput, calls=%fused_computation.44 | convolution fusion | flops 268959744 | bytes 12058624 | tf_op jit(solution)/shard_map/ksm,kmc->ksc/dot_general | solution.py:30
  14.0 1.4 %fusion.57 = bf16[64,32,1,128]{3,1,0,2:T(8,128)(2,1)S(1)} fusion(f32[64,32,128]{2,1,0:T(8,128)S(1)} %fusion, bf16[64,2,512,128]{3,2,1,0:T(8,128)(2,1)S(1)} %copy-done.5, bf16[64,2,32,512]{3,2,1,0:T(8,128)(2,1)S(1)} %copy-done.6), kind=kOutput, calls=%fused_computation.45 | convolution fusion | flops 268959744 | bytes 12058624 | tf_op jit(solution)/shard_map/ksm,kmc->ksc/dot_general | solution.py:30
  15.3 0.1 pad_maximum_fusion
  15.4 0.0 copy-start.3
  15.5 1.4 %copy.45 = bf16[64,32,2,128]{3,0,2,1:T(8,128)(2,1)} copy(bf16[64,32,2,128]{3,1,0,2:T(8,128)(2,1)S(1)} %pad_maximum_fusion) | data formatting | bytes 2097152 | tf_op jit(solution)/shard_map/stack | solution.py:40
  16.9 6.4 %all-to-all-start = ((bf16[64,32,2,128]{3,0,2,1:T(8,128)(2,1)}), bf16[64,32,2,128]{3,0,2,1:T(8,128)(2,1)}, u32[]{:S(2)}, u32[]{:S(2)}) async-start(bf16[64,32,2,128]{3,0,2,1:T(8,128)(2,1)} %copy.45), calls=%async_computation | async-start | bytes 2097152 | tf_op jit(solution)/shard_map/all_to_all | solution.py:45
  23.2 0.1 copy.49
  23.4 0.1 fusion.62
  23.5 0.8 %copy.50 = bf16[1,128,3,128]{3,1,2,0:T(8,128)(2,1)} copy(bf16[1,128,3,128]{1,3,2,0:T(8,128)(2,1)S(1)} %fusion.62) | data formatting | bytes 196608 | tf_op jit(solution)/shard_map/convert_element_type | solution.py:51
  24.2 10.6 %all_gather.4 = bf16[4,128,3,128]{3,1,2,0:T(8,128)(2,1)S(1)} all-gather(bf16[1,128,3,128]{3,1,2,0:T(8,128)(2,1)} %copy.50), channel_id=1, replica_groups=mesh['grp'=4,'freq'=8] {'grp'}, dimensions={0}, use_global_device_ids=true | all-gather | bytes 491520 | tf_op jit(solution)/shard_map/all_gather | solution.py:15
  34.8 0.7 %reduce_sum.12 = bf16[128,3,128]{2,0,1:T(8,128)(2,1)} reduce(bf16[4,128,3,128]{3,1,2,0:T(8,128)(2,1)S(1)} %all_gather.4, bf16[]{:T(256)} %constant.26.clone.1), dimensions={0}, to_apply=%region_0.1 | reduce | flops 147456 | bytes 491522 | tf_op jit(solution)/shard_map/reduce_sum | solution.py:15
  35.5 1.0 %copy.51 = bf16[128,3,128]{0,2,1:T(8,128)(2,1)S(1)} copy(bf16[128,3,128]{2,0,1:T(8,128)(2,1)} %reduce_sum.12) | data formatting | bytes 196608 | tf_op jit(solution)/shard_map/reduce_sum | solution.py:15
  36.5 9.4 %multiply_convert_fusion = (bf16[1,1024,512]{2,1,0:T(8,128)(2,1)}, bf16[1,1024,512]{2,1,0:T(8,128)(2,1)}) fusion(), kind=kLoop, calls=%fused_computation.30 | loop fusion | flops 9961472 | bytes 2097152 | tf_op jit(solution)/shard_map/convert.3
  45.9 4.0 %all-to-all-done = bf16[64,32,2,128]{3,0,2,1:T(8,128)(2,1)} async-done(((bf16[64,32,2,128]{3,0,2,1:T(8,128)(2,1)}), bf16[64,32,2,128]{3,0,2,1:T(8,128)(2,1)}, u32[]{:S(2)}, u32[]{:S(2)}) %all-to-all-start) | async-done | bytes 1048608 | tf_op jit(solution)/shard_map/all_to_all | solution.py:45
  49.9 1.4 %copy.46 = bf16[8,64,4,2,128]{4,1,0,3,2:T(8,128)(2,1)S(1)} copy(bf16[8,64,4,2,128]{4,1,3,2,0:T(8,128)(2,1)} %bitcast.7) | data formatting | bytes 2097152 | tf_op jit(solution)/shard_map/all_to_all | solution.py:45
  51.3 0.1 copy-done.1
  51.4 0.3 copy-done.2
  51.7 2.6 %fusion.31 = f32[4,1024,128]{1,2,0:T(8,128)} fusion(bf16[512,4,2,128]{3,0,2,1:T(8,128)(2,1)S(1)} %bitcast.87, bf16[1,1024,512]{2,1,0:T(8,128)(2,1)S(1)} %copy-done.1, bf16[1,1024,512]{2,1,0:T(8,128)(2,1)S(1)} %copy-done.2), kind=kOutput, calls=%fused_computation.39 | convolution fusion | flops 1074790400 | bytes 5242880 | tf_op jit(solution)/shard_map/qtk,ksqc->stc/dot_general | solution.py:42
  54.3 2.9 %copy.48 = f32[4,1024,128]{2,1,0:T(8,128)} copy(f32[4,1024,128]{1,2,0:T(8,128)} %fusion.31) | data formatting | bytes 4194304 | tf_op jit(solution)/shard_map/qtk,ksqc->stc/transpose | solution.py:42
  57.3 2.9 %copy.52 = f32[4096,128]{0,1:T(8,128)} copy(f32[4096,128]{1,0:T(8,128)} %bitcast.86) | data formatting | bytes 4194304 | tf_op jit(solution)/shard_map/reshape | solution.py:48
  60.2 4.0 %convolution_convert_fusion = bf16[4096,128]{1,0:T(8,128)(2,1)} fusion(bf16[128,128]{1,0:T(8,128)(2,1)S(1)} %copy-done.4, f32[4096,128]{0,1:T(8,128)} %copy.52, bf16[128,384]{0,1:T(8,128)(2,1)S(1)} %bitcast.89, bf16[4096,384]{1,0:T(8,128)(2,1)S(1)} %copy-done), kind=kOutput, calls=%fused_computation.15 | convolution fusion | flops 538443776 | bytes 6422528 | tf_op jit(solution)/shard_map/dot_general | solution.py:57
  (13 shorter events, 0.0 us)
Async XLA Ops:
  0.0 60.2 %copy-start = (bf16[4096,384]{1,0:T(8,128)(2,1)S(1)}, bf16[4096,384]{1,0:T(8,128)(2,1)}, u32[]{:S(2)}) copy-start(bf16[4096,384]{1,0:T(8,128)(2,1)} %param.8) | copy-start | bytes 9437188
  0.0 5.5 %copy-start.6 = (bf16[64,2,32,512]{3,2,1,0:T(8,128)(2,1)S(1)}, bf16[64,2,32,512]{3,2,1,0:T(8,128)(2,1)}, u32[]{:S(2)}) copy-start(bf16[64,2,32,512]{3,2,1,0:T(8,128)(2,1)} %param.6) | copy-start | bytes 12582916
  0.0 12.6 %copy-start.5 = (bf16[64,2,512,128]{3,2,1,0:T(8,128)(2,1)S(1)}, bf16[64,2,512,128]{3,2,1,0:T(8,128)(2,1)}, u32[]{:S(2)}) copy-start(bf16[64,2,512,128]{3,2,1,0:T(8,128)(2,1)} %param.7) | copy-start | bytes 50331652
  15.4 7.8 %copy-start.3 = (bf16[128,384]{1,0:T(8,128)(2,1)S(1)}, bf16[128,384]{1,0:T(8,128)(2,1)}, u32[]{:S(2)}) copy-start(bf16[128,384]{1,0:T(8,128)(2,1)} %param.9) | copy-start | bytes 294916
  15.5 7.9 %copy-start.7 = (s32[3]{0:T(128)S(1)}, s32[3]{0:T(128)}, u32[]{:S(2)}) copy-start(s32[3]{0:T(128)} %param.10) | copy-start | bytes 40
  16.9 33.0 %all-to-all-start = ((bf16[64,32,2,128]{3,0,2,1:T(8,128)(2,1)}), bf16[64,32,2,128]{3,0,2,1:T(8,128)(2,1)}, u32[]{:S(2)}, u32[]{:S(2)}) async-start(bf16[64,32,2,128]{3,0,2,1:T(8,128)(2,1)} %copy.45), calls=%async_computation | async-start | bytes 2097152 | tf_op jit(solution)/shard_map/all_to_all | solution.py:45
  49.9 1.5 %copy-start.1 = (bf16[1,1024,512]{2,1,0:T(8,128)(2,1)S(1)}, bf16[1,1024,512]{2,1,0:T(8,128)(2,1)}, u32[]{:S(2)}) copy-start(bf16[1,1024,512]{2,1,0:T(8,128)(2,1)} %get-tuple-element.5) | copy-start | bytes 3145732
  49.9 1.9 %copy-start.2 = (bf16[1,1024,512]{2,1,0:T(8,128)(2,1)S(1)}, bf16[1,1024,512]{2,1,0:T(8,128)(2,1)}, u32[]{:S(2)}) copy-start(bf16[1,1024,512]{2,1,0:T(8,128)(2,1)} %get-tuple-element.6) | copy-start | bytes 3145732
  57.3 2.9 %copy-start.4 = (bf16[128,128]{1,0:T(8,128)(2,1)S(1)}, bf16[128,128]{1,0:T(8,128)(2,1)}, u32[]{:S(2)}) copy-start(bf16[128,128]{1,0:T(8,128)(2,1)} %param.11) | copy-start | bytes 98308
